TPU v7x, 32 devices: a whole 2x2x4 slice. The times are simulated.
32 devices in a mesh: row: 8 (over z, x), col: 4 (over y, core).
Axes of the slice: x: 2, y: 2, z: 4, core: 2. Of those that a mesh axis runs over, the one named last changes fastest.
Arguments:
- sources_in: bfloat16 [32768, 2, 512], P(('row', 'col')), may hold values from -6 to 6
- right_bases: bfloat16 [64, 8, 2, 96, 512], P(('row', 'col')), may hold values from -0.1875 to 0.1875
- left_bases: bfloat16 [8, 8, 8, 2, 96, 512], P('row', None, 'col'), may hold values from -0.046875 to 0.046875
- tile_ranks: int32 [8, 64], P(None, ('row', 'col')), may hold values from 16 to 96
Outputs:
- redatumed: bfloat16 [4096, 2, 512], P(('row', 'col'))
Inputs may be any that keep to these rules, and one draw needn't show every extreme that they name: `tile_ranks`: each tile's rank; rows of its bases at or beyond it do not count.
All inputs are finite; a program needn't handle non-finite values.
Results may differ from a plain program's by a relative error of at most 0.0049.
Values may be sent and summed in bfloat16 or wider, within the bound.
A program may use at most 256 MiB of HBM per device.

v0:
```python
import jax
import jax.numpy as jnp
from jax import lax
from jax.sharding import PartitionSpec as P


def complex_rows(prod):
    real = prod[:, 0, 0] - prod[:, 1, 1]
    imag = prod[:, 0, 1] + prod[:, 1, 0]
    return jnp.stack([real, imag], 1)


def body(sources_in, right_bases, left_bases, tile_ranks):
    cols, tile_rows, _, rank_pad, width = right_bases.shape
    samples = sources_in.shape[2]
    blocks = sources_in.reshape(cols, width, 2, samples)
    prod = jnp.einsum("cmprb,cbqs->cmpqrs", right_bases, blocks, preferred_element_type=jnp.float32)
    real = prod[:, :, 0, 0] - prod[:, :, 1, 1]
    imag = prod[:, :, 0, 1] + prod[:, :, 1, 0]
    levels = lax.broadcasted_iota(jnp.int32, (cols, tile_rows, rank_pad), 2)
    keep = (levels < tile_ranks.T[:, :, None]).astype(jnp.float32)
    coeffs = (jnp.stack([real, imag], 2) * keep[:, :, None, :, None]).astype(jnp.bfloat16)
    left_flat = left_bases.reshape(-1, 2, rank_pad, width)
    picked = lax.all_to_all(coeffs, "row", split_axis=1, concat_axis=0, tiled=True)[:, 0]
    terms = jnp.einsum("jpkb,jqks->bpqs", left_flat, picked, preferred_element_type=jnp.float32)
    partial_value = complex_rows(terms)
    return lax.psum_scatter(partial_value, "col", scatter_dimension=0, tiled=True).astype(
        jnp.bfloat16
    )


def solution(mesh):
    in_specs = (
        P(("row", "col"), None, None),
        P(("row", "col"), None, None, None, None),
        P("row", None, "col", None, None, None),
        P(None, ("row", "col")),
    )
    out_specs = P(("row", "col"), None, None)
    return jax.shard_map(body, mesh=mesh, in_specs=in_specs, out_specs=out_specs, check_vma=False)
```

profile of v0, /device:TPU:0, one launch (start us, length us, event | category | flops | bytes accessed | tf_op | source)
XLA Modules:
  0.0 140.6 jit_solution(18144170342708530463)
XLA Ops:
  6.5 0.0 copy-start
  6.5 0.0 reduce-scatter.2.cloned.1.call-start
  6.5 1.9 %copy-done = bf16[2,8,2,96,512]{4,3,2,1,0:T(8,128)(2,1)S(1)} copy-done((bf16[2,8,2,96,512]{4,3,2,1,0:T(8,128)(2,1)S(1)}, bf16[2,8,2,96,512]{4,3,2,1,0:T(8,128)(2,1)}, u32[]{:S(2)}) %copy-start) | copy-done | bytes 3145752
  8.4 5.0 %convolution_bitcast_fusion = f32[2,8,2,2,96,512]{5,4,2,1,3,0:T(8,128)S(1)} fusion(bf16[2,8,2,96,512]{4,3,2,1,0:T(8,128)(2,1)S(1)} %copy-done, bf16[2,512,2,512,1,1]{3,2,1,0,5,4:T(2,128)(2,1)} %bitcast.60), kind=kOutput, calls=%fused_computation.2 | convolution fusion | flops 3221225472 | bytes 17825792 | tf_op jit(solution)/shard_map/cmprb,cbqs->cmpqrs/dot_general | solution.py:17
  13.4 0.9 fusion.1
  14.3 0.0 copy-start.1
  14.3 0.9 fusion.3
  15.2 0.0 copy-done.1
  15.2 0.1 fusion.18
  15.3 0.5 fusion
  15.8 0.3 copy.24
  16.1 77.8 %all_to_all.15 = bf16[2,8,2,96,512]{4,3,0,2,1:T(8,128)(2,1)S(1)} all-to-all(bf16[2,8,2,96,512]{4,3,0,2,1:T(8,128)(2,1)S(1)} %copy.24), channel_id=1, replica_groups=mesh['row'=8,'col'=4] {'row'}, dimensions={1} | all-to-all | bytes 6291456 | tf_op jit(solution)/shard_map/all_to_all | solution.py:24
  93.9 0.0 copy-start.2
  93.9 0.3 copy.25
  94.2 1.6 %copy-done.2 = bf16[1,8,2,2,96,512]{5,4,3,2,1,0:T(8,128)(2,1)S(1)} copy-done((bf16[1,8,2,2,96,512]{5,4,3,2,1,0:T(8,128)(2,1)S(1)}, bf16[1,8,2,2,96,512]{5,4,3,2,1,0:T(8,128)(2,1)}, u32[]{:S(2)}) %copy-start.2) | copy-done | bytes 3145752
  95.8 3.5 %fusion.9 = f32[512,2,2,512]{0,3,1,2:T(8,128)S(1)} fusion(bf16[16,2,96,512]{3,2,1,0:T(8,128)(2,1)S(1)} %bitcast.59, bf16[16,2,96,512,1]{3,2,1,0,4:T(8,128)(2,1)S(1)} %bitcast.57), kind=kOutput, calls=%fused_computation.14 | convolution fusion | flops 3221225472 | bytes 10485760 | tf_op jit(solution)/shard_map/jpkb,jqks->bpqs/dot_general | solution.py:25
  99.2 0.2 fusion.15
  99.4 0.2 fusion.17
  99.7 1.5 %pad_maximum_fusion = f32[512,2,512]{0,2,1:T(8,128)} fusion(f32[512,1,512]{0,2,1:T(8,128)S(1)} %fusion.15, f32[512,1,512]{0,2,1:T(8,128)S(1)} %fusion.17), kind=kLoop, calls=%fused_computation.15 | loop fusion | flops 524288 | bytes 4194304 | tf_op jit(solution)/shard_map/stack | solution.py:10
  101.2 0.0 reduce-scatter.2.cloned.1.call-update
  101.2 30.6 %reduce-scatter.2.cloned.1.call-done = f32[128,2,512]{0,2,1:T(8,128)} async-done(((f32[512,2,512]{0,2,1:T(8,128)}), f32[128,2,512]{0,2,1:T(8,128)}) %reduce-scatter.2.cloned.1.call-update) | async-done | bytes 524304 | tf_op jit(solution)/shard_map/reduce_scatter | solution.py:27
  131.8 1.1 convert_element_type.15
  132.9 0.9 copy.30
Async XLA Ops:
  6.5 1.9 %copy-start = (bf16[2,8,2,96,512]{4,3,2,1,0:T(8,128)(2,1)S(1)}, bf16[2,8,2,96,512]{4,3,2,1,0:T(8,128)(2,1)}, u32[]{:S(2)}) copy-start(bf16[2,8,2,96,512]{4,3,2,1,0:T(8,128)(2,1)} %param.5) | copy-start | bytes 9437188
  6.5 125.2 %reduce-scatter.2.cloned.1.call-start = ((), (), s32[]{:S(2)}) async-start(), calls=%async_computation.2 | async-start | bytes 2621440 | tf_op jit(solution)/shard_map/reduce_scatter | solution.py:27
  14.3 0.9 copy-start.1
  93.9 1.9 %copy-start.2 = (bf16[1,8,2,2,96,512]{5,4,3,2,1,0:T(8,128)(2,1)S(1)}, bf16[1,8,2,2,96,512]{5,4,3,2,1,0:T(8,128)(2,1)}, u32[]{:S(2)}) copy-start(bf16[1,8,2,2,96,512]{5,4,3,2,1,0:T(8,128)(2,1)} %param.6) | copy-start | bytes 9437188
Sparse Core Ops, SparseCore 0:
  101.3 30.4 reduce-scatter.1
where the time goes:
time: 141 us
  blocking collectives  77.8 us (55%)
  waiting for transfers between devices  30.6 us (22%)
  between operations  13.5 us (10%)
  matrix products  8.46 us (6%)
  other arithmetic  5.29 us (4%)
  local copies, waits for them, and re-layouts  4.98 us (4%)
    all_to_all x1, blocking collectives, body(): lax.all_to_all(coeffs, 'row', split_axis=1, concat_axis=0, tiled=True)[:, 0]  77.8 us
    reduce_scatter x1, waiting for transfers between devices, body(): lax.psum_scatter(partial_value, 'col', scatter_dimension=0, tiled=True)  30.6 us
    dot_general x1, matrix products, body(): jnp.einsum('cmprb,cbqs->cmpqrs', right_bases, blocks, preferred_element_t...  5 us
    dot_general x1, matrix products, body(): jnp.einsum('jpkb,jqks->bpqs', left_flat, picked, preferred_element_type=j...  3.46 us
    unnamed x6, local copies, waits for them, and re-layouts  3.46 us
  transfers between devices with their start and end apart: 1, of which 1 were waited for; matrix products, arithmetic and copies ran while one was open for 0% of the time, Pallas kernels for 0%

commit v1 on v0

--- a/solution.py
+++ b/solution.py
@@ -21,7 +21,10 @@
     keep = (levels < tile_ranks.T[:, :, None]).astype(jnp.float32)
     coeffs = (jnp.stack([real, imag], 2) * keep[:, :, None, :, None]).astype(jnp.bfloat16)
     left_flat = left_bases.reshape(-1, 2, rank_pad, width)
-    picked = lax.all_to_all(coeffs, "row", split_axis=1, concat_axis=0, tiled=True)[:, 0]
+    picked = jnp.concatenate(
+        lax.all_to_all(jnp.stack(jnp.split(coeffs, lax.axis_size("row"), axis=1)), "row", 0, 0),
+        axis=0,
+    )[:, 0]
     terms = jnp.einsum("jpkb,jqks->bpqs", left_flat, picked, preferred_element_type=jnp.float32)
     partial_value = complex_rows(terms)
     return lax.psum_scatter(partial_value, "col", scatter_dimension=0, tiled=True).astype(

time: 141 us -> 141 us (level)
    unnamed x6 -> x13, local copies, waits for them, and re-layouts: 3.46 us -> 3.65 us
where the time goes in v1:
time: 141 us
  blocking collectives  77.8 us (55%)
  waiting for transfers between devices  30.6 us (22%)
  between operations  13.5 us (10%)
  matrix products  8.46 us (6%)
  other arithmetic  5.29 us (4%)
  local copies, waits for them, and re-layouts  4.88 us (3%)
    all_to_all x1, blocking collectives, body(): lax.all_to_all(jnp.stack(jnp.split(coeffs, lax.axis_size('row'), axis=1))...  77.8 us
    reduce_scatter x1, waiting for transfers between devices, body(): lax.psum_scatter(partial_value, 'col', scatter_dimension=0, tiled=True)  30.6 us
    dot_general x1, matrix products, body(): jnp.einsum('cmprb,cbqs->cmpqrs', right_bases, blocks, preferred_element_t...  5 us
    unnamed x13, local copies, waits for them, and re-layouts  3.65 us
    dot_general x1, matrix products, body(): jnp.einsum('jpkb,jqks->bpqs', left_flat, picked, preferred_element_type=j...  3.46 us
  transfers between devices with their start and end apart: 1, of which 1 were waited for; matrix products, arithmetic and copies ran while one was open for 0% of the time, Pallas kernels for 0%

profile of v1, /device:TPU:0, one launch (start us, length us, event | category | flops | bytes accessed | tf_op | source)
XLA Modules:
  0.0 140.5 jit_solution(3118832098388239922)
XLA Ops:
  6.5 0.0 copy-start
  6.5 0.0 reduce-scatter.2.cloned.1.call-start
  6.5 1.9 %copy-done = bf16[2,8,2,96,512]{4,3,2,1,0:T(8,128)(2,1)S(1)} copy-done((bf16[2,8,2,96,512]{4,3,2,1,0:T(8,128)(2,1)S(1)}, bf16[2,8,2,96,512]{4,3,2,1,0:T(8,128)(2,1)}, u32[]{:S(2)}) %copy-start) | copy-done | bytes 3145752
  8.4 5.0 %convolution_bitcast_fusion = f32[2,8,2,2,96,512]{5,4,2,1,3,0:T(8,128)S(1)} fusion(bf16[2,8,2,96,512]{4,3,2,1,0:T(8,128)(2,1)S(1)} %copy-done, bf16[2,512,2,512,1,1]{3,2,1,0,5,4:T(2,128)(2,1)} %bitcast.102), kind=kOutput, calls=%fused_computation.2 | convolution fusion | flops 3221225472 | bytes 17825792 | tf_op jit(solution)/shard_map/cmprb,cbqs->cmpqrs/dot_general | solution.py:17
  13.4 0.9 fusion.1
  14.3 0.0 copy-start.1
  14.3 0.9 fusion.3
  15.2 0.0 copy-done.1
  15.2 0.1 fusion.26
  15.3 0.5 fusion
  16.1 77.8 %all_to_all.5 = bf16[8,2,1,2,96,512]{5,4,1,3,2,0:T(8,128)(2,1)S(1)} all-to-all(bf16[8,2,1,2,96,512]{5,4,1,3,2,0:T(8,128)(2,1)S(1)} %fusion.18), channel_id=1, replica_groups=mesh['row'=8,'col'=4] {'row'}, dimensions={0} | all-to-all | bytes 6291456 | tf_op jit(solution)/shard_map/all_to_all | solution.py:25
  93.8 0.0 copy-start.2
  93.8 0.3 copy.29
  94.1 1.6 %copy-done.2 = bf16[1,8,2,2,96,512]{5,4,3,2,1,0:T(8,128)(2,1)S(1)} copy-done((bf16[1,8,2,2,96,512]{5,4,3,2,1,0:T(8,128)(2,1)S(1)}, bf16[1,8,2,2,96,512]{5,4,3,2,1,0:T(8,128)(2,1)}, u32[]{:S(2)}) %copy-start.2) | copy-done | bytes 3145752
  95.7 3.5 %fusion.9 = f32[512,2,2,512]{0,3,1,2:T(8,128)S(1)} fusion(bf16[16,2,96,512]{3,2,1,0:T(8,128)(2,1)S(1)} %bitcast.101, bf16[16,2,96,512,1]{3,2,1,0,4:T(8,128)(2,1)S(1)} %bitcast.99), kind=kOutput, calls=%fused_computation.14 | convolution fusion | flops 3221225472 | bytes 10485760 | tf_op jit(solution)/shard_map/jpkb,jqks->bpqs/dot_general | solution.py:28
  99.2 0.2 fusion.15
  99.4 0.2 fusion.17
  99.6 1.5 %pad_maximum_fusion = f32[512,2,512]{0,2,1:T(8,128)} fusion(f32[512,1,512]{0,2,1:T(8,128)S(1)} %fusion.15, f32[512,1,512]{0,2,1:T(8,128)S(1)} %fusion.17), kind=kLoop, calls=%fused_computation.15 | loop fusion | flops 524288 | bytes 4194304 | tf_op jit(solution)/shard_map/stack | solution.py:10
  101.1 0.0 reduce-scatter.2.cloned.1.call-update
  101.1 30.6 %reduce-scatter.2.cloned.1.call-done = f32[128,2,512]{0,2,1:T(8,128)} async-done(((f32[512,2,512]{0,2,1:T(8,128)}), f32[128,2,512]{0,2,1:T(8,128)}) %reduce-scatter.2.cloned.1.call-update) | async-done | bytes 524304 | tf_op jit(solution)/shard_map/reduce_scatter | solution.py:30
  131.7 1.1 convert_element_type.15
  132.8 0.9 copy.34
  (8 shorter events, 0.2 us)
Async XLA Ops:
  6.5 1.9 %copy-start = (bf16[2,8,2,96,512]{4,3,2,1,0:T(8,128)(2,1)S(1)}, bf16[2,8,2,96,512]{4,3,2,1,0:T(8,128)(2,1)}, u32[]{:S(2)}) copy-start(bf16[2,8,2,96,512]{4,3,2,1,0:T(8,128)(2,1)} %param.5) | copy-start | bytes 9437188
  6.5 125.2 %reduce-scatter.2.cloned.1.call-start = ((), (), s32[]{:S(2)}) async-start(), calls=%async_computation.2 | async-start | bytes 2621440 | tf_op jit(solution)/shard_map/reduce_scatter | solution.py:30
  14.3 0.9 copy-start.1
  93.8 1.9 %copy-start.2 = (bf16[1,8,2,2,96,512]{5,4,3,2,1,0:T(8,128)(2,1)S(1)}, bf16[1,8,2,2,96,512]{5,4,3,2,1,0:T(8,128)(2,1)}, u32[]{:S(2)}) copy-start(bf16[1,8,2,2,96,512]{5,4,3,2,1,0:T(8,128)(2,1)} %param.6) | copy-start | bytes 9437188
Sparse Core Ops, SparseCore 0:
  101.3 30.4 reduce-scatter.1
